TPU v7x, 32 devices: a whole 2x2x4 slice. The times are simulated.
32 devices in a mesh: ctx: 16 (over z, y, x), fsdp: 2 (over core).
Axes of the slice: x: 2, y: 2, z: 4, core: 2. Of those that a mesh axis runs over, the one named last changes fastest.
Arguments:
- inputs: bfloat16 [2, 2048, 1024], P('fsdp', 'ctx'), may hold values from -48 to 48
- cotangent: bfloat16 [2, 2048, 1024], P('fsdp', 'ctx'), may hold values from -6 to 6
- doc_lengths: int32 [2, 8], P('fsdp'), may hold values from 1 to 1024, 2048 in all within a row
- qkv_weight: bfloat16 [1024, 3072], P('fsdp'), may hold values from -0.1875 to 0.1875
- out_weight: bfloat16 [1024, 1024], P('fsdp'), may hold values from -0.1875 to 0.1875
- fc1_weight: bfloat16 [1024, 4096], P('fsdp'), may hold values from -0.1875 to 0.1875
- fc2_weight: bfloat16 [4096, 1024], P('fsdp'), may hold values from -0.09375 to 0.09375
- norm_gain: bfloat16 [3, 1024], P(None, 'fsdp'), may hold values from 0.099609375 to 1.8984375
- norm_bias: bfloat16 [3, 1024], P(None, 'fsdp'), may hold values from -1.5 to 1.5
- mid_gain: bfloat16 [4096], P('fsdp'), may hold values from 0.099609375 to 1.8984375
- mid_bias: bfloat16 [4096], P('fsdp'), may hold values from -1.5 to 1.5
- head_scale: bfloat16 [16], P('fsdp'), may hold values from 0.5 to 2
Outputs:
- output: bfloat16 [2, 2048, 1024], P('fsdp', 'ctx')
- input_grad: bfloat16 [2, 2048, 1024], P('fsdp', 'ctx')
- qkv_grad: float32 [1024, 3072], P('fsdp')
- out_grad: float32 [1024, 1024], P('fsdp')
- fc1_grad: float32 [1024, 4096], P('fsdp')
- fc2_grad: float32 [4096, 1024], P('fsdp')
- gain_grad: float32 [3, 1024], P(None, 'fsdp')
- bias_grad: float32 [3, 1024], P(None, 'fsdp')
- mid_gain_grad: float32 [4096], P('fsdp')
- mid_bias_grad: float32 [4096], P('fsdp')
- scale_grad: float32 [16], P('fsdp')
- rms_values: float32 [3], replicated
Inputs may be any that keep to these rules, and one draw needn't show every extreme that they name: `doc_lengths`: each row holds 8 document lengths that sum to 2048; the longest is 1024.
All inputs are finite; a program needn't handle non-finite values.
Results may differ from a plain program's by a relative error of at most 0.022.
Values may be sent and summed in bfloat16 or wider, within the bound.
No kernel may reach another device: no remote copies, remote signals or barrier semaphores. Data moves between devices by JAX's collectives and lax.ppermute only.
A program may use at most 320 MiB of HBM per device.

v0:
```python
from functools import partial
import math
import jax
import jax.numpy as jnp
from jax import lax
from jax.sharding import PartitionSpec as P

HEADS = 16
HEAD_DIM = 64
epsilon = 1e-05
masked_value = -1e30


def stored_positions(first_row, n_rows, half_rows, groups):
    offsets = first_row + jnp.arange(n_rows, dtype=jnp.int32)
    halves = offsets // half_rows
    paired = halves // 2
    placed = jnp.where(halves % 2 == 0, paired, 2 * groups - 1 - paired)
    return placed * half_rows + offsets % half_rows


def doc_floor(positions, starts):
    begun_mask = starts[None, :] <= positions[:, None]
    return jnp.max(jnp.where(begun_mask, starts[None, :], 0), axis=1)


def allowed_mask(query_pos, query_floor, key_pos):
    return (key_pos[None, :] <= query_pos[:, None]) & (key_pos[None, :] >= query_floor[:, None])


def normalize(values):
    centered = values - jnp.mean(values, axis=-1, keepdims=True)
    inverse = lax.rsqrt(jnp.mean(centered * centered, axis=-1, keepdims=True) + epsilon)
    return (centered * inverse, inverse)


def norm_backward(grad_out, normed, inverse, gain_vec):
    grad_normed = grad_out * gain_vec
    grad_in = inverse * (
        grad_normed
        - jnp.mean(grad_normed, axis=-1, keepdims=True)
        - normed * jnp.mean(grad_normed * normed, axis=-1, keepdims=True)
    )
    return (grad_in, jnp.sum(grad_out * normed, axis=0), jnp.sum(grad_out, axis=0))


def split_heads(rows_array, model_width):
    n_rows = rows_array.shape[0]
    return (
        rows_array[:, :model_width].reshape(n_rows, HEADS, HEAD_DIM),
        rows_array[:, model_width:].reshape(n_rows, HEADS, HEAD_DIM),
    )


def block_grads(query_heads, dout_heads, log_total, delta_rows, key_heads, value_heads, allowed):
    scores = jnp.einsum(
        "qhe,khe->qhk", query_heads, key_heads, preferred_element_type=jnp.float32
    ) * HEAD_DIM ** (-0.5)
    p_block = jnp.where(allowed[:, None, :], jnp.exp(scores - log_total[:, :, None]), 0.0)
    grad_probs = jnp.einsum(
        "qhe,khe->qhk", dout_heads, value_heads, preferred_element_type=jnp.float32
    )
    grad_scores = (p_block * (grad_probs - delta_rows[:, :, None])).astype(jnp.bfloat16)
    return (grad_scores, p_block.astype(jnp.bfloat16))


def local(
    inputs,
    cotangent,
    doc_lengths,
    qkv_weight,
    out_weight,
    fc1_weight,
    fc2_weight,
    norm_gain,
    norm_bias,
    mid_gain,
    mid_bias,
    head_scale,
):
    groups = lax.axis_size("ctx")
    member = lax.axis_index("ctx")
    x_local = inputs[0].astype(jnp.float32)
    tok_rows, model_width = x_local.shape
    half_rows = tok_rows // 2
    stream_rows = tok_rows * groups
    score_scale = HEAD_DIM ** (-0.5)
    (
        qkv_full,
        out_full,
        fc1_full,
        fc2_full,
        gain_full,
        bias_full,
        mid_gain_full,
        mid_bias_full,
        scale_full,
    ) = (
        lax.all_gather(qkv_weight, "fsdp", axis=0, tiled=True),
        lax.all_gather(out_weight, "fsdp", axis=0, tiled=True),
        lax.all_gather(fc1_weight, "fsdp", axis=0, tiled=True),
        lax.all_gather(fc2_weight, "fsdp", axis=0, tiled=True),
        lax.all_gather(norm_gain, "fsdp", axis=1, tiled=True),
        lax.all_gather(norm_bias, "fsdp", axis=1, tiled=True),
        lax.all_gather(mid_gain, "fsdp", axis=0, tiled=True),
        lax.all_gather(mid_bias, "fsdp", axis=0, tiled=True),
        lax.all_gather(head_scale, "fsdp", axis=0, tiled=True),
    )
    norm_gains = gain_full.astype(jnp.float32)
    norm_biases = bias_full.astype(jnp.float32)
    mid_gains = mid_gain_full.astype(jnp.float32)
    mid_biases = mid_bias_full.astype(jnp.float32)
    head_scales = scale_full.astype(jnp.float32)
    lengths_row = doc_lengths[0]
    starts = jnp.cumsum(lengths_row) - lengths_row
    my_pos = stored_positions(member * tok_rows, tok_rows, half_rows, groups)
    my_floor = doc_floor(my_pos, starts)
    norm_one, inv_one = normalize(x_local)
    normed_one = (norm_one * norm_gains[0] + norm_biases[0]).astype(jnp.bfloat16)
    project = jnp.dot(normed_one, qkv_full, preferred_element_type=jnp.float32).astype(jnp.bfloat16)
    queries = project[:, :model_width].reshape(tok_rows, HEADS, HEAD_DIM)
    keys_values = project[:, model_width:]
    start_state = (
        jnp.zeros((tok_rows, HEADS, HEAD_DIM), jnp.float32),
        jnp.full((tok_rows, HEADS), masked_value, jnp.float32),
        jnp.zeros((tok_rows, HEADS), jnp.float32),
    )
    running = start_state
    fetched = lax.all_gather(keys_values, "ctx", axis=0, tiled=True)
    n_rows = fetched.shape[0]
    sub_rows = math.gcd(n_rows, 1024)
    fetched_blocks = fetched.reshape(n_rows // sub_rows, sub_rows, 2 * model_width)
    block_firsts = sub_rows * jnp.arange(n_rows // sub_rows, dtype=jnp.int32)

    def attend_block(state_now, scanned):
        out_sum, row_max, row_sum = state_now
        key_block, block_first = scanned
        key_heads, value_heads = split_heads(key_block, model_width)
        key_pos = stored_positions(block_first, sub_rows, half_rows, groups)
        usable = allowed_mask(my_pos, my_floor, key_pos)[:, None, :]
        scores = (
            jnp.einsum("qhe,khe->qhk", queries, key_heads, preferred_element_type=jnp.float32)
            * score_scale
        )
        new_max = jnp.maximum(row_max, jnp.max(jnp.where(usable, scores, masked_value), axis=-1))
        p_block = jnp.where(usable, jnp.exp(scores - new_max[:, :, None]), 0.0)
        rescale = jnp.exp(row_max - new_max)
        row_sum = row_sum * rescale + jnp.sum(p_block, axis=-1)
        out_sum = out_sum * rescale[:, :, None] + jnp.einsum(
            "qhk,khe->qhe",
            p_block.astype(jnp.bfloat16),
            value_heads,
            preferred_element_type=jnp.float32,
        )
        return ((out_sum, new_max, row_sum), None)

    running, unused_out = lax.scan(attend_block, running, (fetched_blocks, block_firsts))
    out_sum, row_max, row_sum = running
    attended = out_sum / row_sum[:, :, None]
    log_total = row_max + jnp.log(row_sum)
    scaled = (
        (attended * head_scales[None, :, None]).reshape(tok_rows, model_width).astype(jnp.bfloat16)
    )
    branch = jnp.dot(scaled, out_full, preferred_element_type=jnp.float32)
    norm_att, inv_att = normalize(branch)
    attn_out = norm_att * norm_gains[1] + norm_biases[1]
    middle = x_local + attn_out
    norm_two, inv_two = normalize(middle)
    normed_two = (norm_two * norm_gains[2] + norm_biases[2]).astype(jnp.bfloat16)
    hidden = jnp.dot(normed_two, fc1_full, preferred_element_type=jnp.float32)
    active, gelu_back = jax.vjp(partial(jax.nn.gelu, approximate=True), hidden)
    norm_mid, inv_mid = normalize(active)
    mixed_in = (norm_mid * mid_gains + mid_biases).astype(jnp.bfloat16)
    ffn_out = jnp.dot(mixed_in, fc2_full, preferred_element_type=jnp.float32)
    result = middle + ffn_out
    sq_sums = lax.psum(
        jnp.stack(
            [jnp.sum(result * result), jnp.sum(attn_out * attn_out), jnp.sum(ffn_out * ffn_out)]
        ),
        ("ctx", "fsdp"),
    )
    rms_values = jnp.sqrt(sq_sums / (stream_rows * lax.axis_size("fsdp") * model_width))
    grad_top = cotangent[0].astype(jnp.float32)
    grad_ffn = cotangent[0]
    fc2_grad = jnp.einsum("tf,td->fd", mixed_in, grad_ffn, preferred_element_type=jnp.float32)
    grad_mixed = jnp.einsum("td,fd->tf", grad_ffn, fc2_full, preferred_element_type=jnp.float32)
    grad_active, mid_gain_grad, mid_bias_grad = norm_backward(
        grad_mixed, norm_mid, inv_mid, mid_gains
    )
    grad_hidden = gelu_back(grad_active)[0].astype(jnp.bfloat16)
    fc1_grad = jnp.einsum("td,tf->df", normed_two, grad_hidden, preferred_element_type=jnp.float32)
    grad_two = jnp.einsum("tf,df->td", grad_hidden, fc1_full, preferred_element_type=jnp.float32)
    grad_mid_in, gain_two, bias_two = norm_backward(grad_two, norm_two, inv_two, norm_gains[2])
    grad_middle = grad_top + grad_mid_in
    grad_branch_f, gain_att, bias_att = norm_backward(grad_middle, norm_att, inv_att, norm_gains[1])
    grad_branch = grad_branch_f.astype(jnp.bfloat16)
    out_grad = jnp.einsum("ta,tb->ab", scaled, grad_branch, preferred_element_type=jnp.float32)
    grad_scaled = jnp.einsum(
        "tb,ab->ta", grad_branch, out_full, preferred_element_type=jnp.float32
    ).reshape(tok_rows, HEADS, HEAD_DIM)
    scale_grad = jnp.sum(grad_scaled * attended, axis=(0, 2))
    grad_att = (grad_scaled * head_scales[None, :, None]).astype(jnp.bfloat16)
    delta_rows = jnp.sum(grad_att.astype(jnp.float32) * attended, axis=-1)
    query_start = jnp.zeros((tok_rows, HEADS, HEAD_DIM), jnp.float32)
    every_kv = lax.all_gather(keys_values, "ctx", axis=0, tiled=True)
    running = query_start
    n_rows = every_kv.shape[0]
    query_sub_rows = math.gcd(n_rows, 1024)
    fetched_blocks = every_kv.reshape(n_rows // query_sub_rows, query_sub_rows, 2 * model_width)
    block_firsts = 0 + query_sub_rows * jnp.arange(n_rows // query_sub_rows, dtype=jnp.int32)

    def query_block(partial_sum, scanned):
        key_block, block_first = scanned
        key_heads, value_heads = split_heads(key_block, model_width)
        key_pos = stored_positions(block_first, query_sub_rows, half_rows, groups)
        allowed = allowed_mask(my_pos, my_floor, key_pos)
        grad_scores, unused_low = block_grads(
            queries, grad_att, log_total, delta_rows, key_heads, value_heads, allowed
        )
        return (
            partial_sum
            + jnp.einsum(
                "qhk,khe->qhe", grad_scores, key_heads, preferred_element_type=jnp.float32
            ),
            None,
        )

    running, unused_out = lax.scan(query_block, running, (fetched_blocks, block_firsts))
    n_rows = tok_rows * lax.axis_size("ctx")
    key_sub_rows = math.gcd(n_rows, 1024)

    def key_term(sub_first):
        key_block = lax.dynamic_slice_in_dim(every_kv, sub_first, key_sub_rows, 0)
        key_heads, value_heads = split_heads(key_block, model_width)
        key_pos = stored_positions(sub_first, key_sub_rows, half_rows, groups)
        allowed = allowed_mask(my_pos, my_floor, key_pos)
        grad_scores, low_probs = block_grads(
            queries, grad_att, log_total, delta_rows, key_heads, value_heads, allowed
        )
        grad_keys = (
            jnp.einsum("qhk,qhe->khe", grad_scores, queries, preferred_element_type=jnp.float32)
            * score_scale
        )
        grad_values = jnp.einsum(
            "qhk,qhe->khe", low_probs, grad_att, preferred_element_type=jnp.float32
        )
        return jnp.concatenate(
            [
                grad_keys.reshape(key_sub_rows, model_width),
                grad_values.reshape(key_sub_rows, model_width),
            ],
            axis=1,
        )

    sub_firsts = key_sub_rows * jnp.arange(n_rows // key_sub_rows, dtype=jnp.int32)
    kv_grad = lax.psum_scatter(
        lax.map(key_term, sub_firsts).reshape(n_rows, 2 * model_width),
        "ctx",
        scatter_dimension=0,
        tiled=True,
    )
    grad_queries = (running * score_scale).reshape(tok_rows, model_width)
    grad_project = jnp.concatenate([grad_queries, kv_grad], axis=1).astype(jnp.bfloat16)
    qkv_grad = jnp.einsum("td,tp->dp", normed_one, grad_project, preferred_element_type=jnp.float32)
    grad_one = jnp.einsum("tp,dp->td", grad_project, qkv_full, preferred_element_type=jnp.float32)
    grad_first, gain_one, bias_one = norm_backward(grad_one, norm_one, inv_one, norm_gains[0])
    input_grad = (grad_middle + grad_first).astype(jnp.bfloat16)[None]
    gain_grad = jnp.stack([gain_one, gain_att, gain_two])
    bias_grad = jnp.stack([bias_one, bias_att, bias_two])
    shard_grads = (
        lax.psum_scatter(
            qkv_grad.astype(jnp.bfloat16), "fsdp", scatter_dimension=0, tiled=True
        ).astype(jnp.float32),
        lax.psum_scatter(
            out_grad.astype(jnp.bfloat16), "fsdp", scatter_dimension=0, tiled=True
        ).astype(jnp.float32),
        lax.psum_scatter(
            fc1_grad.astype(jnp.bfloat16), "fsdp", scatter_dimension=0, tiled=True
        ).astype(jnp.float32),
        lax.psum_scatter(
            fc2_grad.astype(jnp.bfloat16), "fsdp", scatter_dimension=0, tiled=True
        ).astype(jnp.float32),
        lax.psum_scatter(
            gain_grad.astype(jnp.bfloat16), "fsdp", scatter_dimension=1, tiled=True
        ).astype(jnp.float32),
        lax.psum_scatter(
            bias_grad.astype(jnp.bfloat16), "fsdp", scatter_dimension=1, tiled=True
        ).astype(jnp.float32),
        lax.psum_scatter(
            mid_gain_grad.astype(jnp.bfloat16), "fsdp", scatter_dimension=0, tiled=True
        ).astype(jnp.float32),
        lax.psum_scatter(
            mid_bias_grad.astype(jnp.bfloat16), "fsdp", scatter_dimension=0, tiled=True
        ).astype(jnp.float32),
        lax.psum_scatter(
            scale_grad.astype(jnp.bfloat16), "fsdp", scatter_dimension=0, tiled=True
        ).astype(jnp.float32),
    )
    summed = lax.psum(
        (
            shard_grads[0],
            shard_grads[1],
            shard_grads[2],
            shard_grads[3],
            shard_grads[4],
            shard_grads[5],
            shard_grads[6],
            shard_grads[7],
            shard_grads[8],
        ),
        "ctx",
    )
    return (
        result.astype(jnp.bfloat16)[None],
        input_grad,
        summed[0],
        summed[1],
        summed[2],
        summed[3],
        summed[4],
        summed[5],
        summed[6],
        summed[7],
        summed[8],
        rms_values,
    )


def solution(mesh):
    placed = (
        P("fsdp", "ctx", None),
        P("fsdp", "ctx", None),
        P("fsdp", None),
        P("fsdp", None),
        P("fsdp", None),
        P("fsdp", None),
        P("fsdp", None),
        P(None, "fsdp"),
        P(None, "fsdp"),
        P("fsdp"),
        P("fsdp"),
        P("fsdp"),
    )
    return jax.shard_map(
        local,
        mesh=mesh,
        in_specs=placed,
        out_specs=(
            P("fsdp", "ctx", None),
            P("fsdp", "ctx", None),
            P("fsdp", None),
            P("fsdp", None),
            P("fsdp", None),
            P("fsdp", None),
            P(None, "fsdp"),
            P(None, "fsdp"),
            P("fsdp"),
            P("fsdp"),
            P("fsdp"),
            P(),
        ),
        check_vma=False,
    )
```

profile of v0, /device:TPU:26, one launch (start us, length us, event | category | flops | bytes accessed | tf_op | source)
XLA Modules:
  0.0 1870.3 jit_solution(4212419879417016194)
XLA Ops:
  12.1 15.5 all-gather.6.cloned.1.call-done
  43.0 100.6 %all-gather.8.cloned.1.call-done = bf16[2048,2048]{1,0:T(8,128)(2,1)} async-done(((bf16[128,2048]{1,0:T(8,128)(2,1)}), bf16[2048,2048]{1,0:T(8,128)(2,1)}) %all-gather.8.cloned.1.call-update) | async-done | bytes 8388624 | tf_op jit(solution)/shard_map/all_gather | solution.py:129
  143.6 12.0 copy.75
  155.7 40.6 %while.47 = (s32[]{:T(128)}, f32[128,16,64]{0,2,1:T(8,128)S(1)}, f32[128,16]{0,1:T(8,128)S(1)}, f32[128,16]{0,1:T(8,128)S(1)}, s32[2]{0:T(128)S(1)}, /*index=5*/...) while((s32[]{:T(128)}, f32[128,16,64]{0,2,1:T(8,128)S(1)}, ...), condition=%wide.region_7.8_spmd.clone, body=%wide.region_4.7_spmd.clone.sunk | while | flops 560786944 | bytes 81667752 | solution.py:157
  165.5 6.6 fusion.229
  185.8 6.3 fusion.229
  200.8 5.5 fusion.131
  207.5 6.7 multiply_reduce_fusion
  216.3 6.7 fusion.143
  230.1 116.8 %while.46 = (s32[]{:T(128)}, f32[2,1024,2048]{2,1,0:T(8,128)}, s32[2]{0:T(128)S(1)}, s32[128]{0:T(128)S(1)}, bf16[2048,2048]{1,0:T(8,128)(2,1)}, /*index=5*/bf16...) while((s32[]{:T(128)}, f32[2,1024,2048]{2,1,0:T(8,128)}, ...), condition=%wide.region_24.25_spmd.clone, body=%wide.region_23.24_spmd.clone.sunk | while | flops 1098302976 | bytes 123111664 | solution.py:257
  233.2 5.3 fusion.216
  242.4 6.3 fusion.217
  252.3 10.0 broadcast_multiply_fusion.14
  262.2 5.4 fusion.220
  271.9 9.1 copy.129
  281.0 7.7 constant_dynamic-update-slice_fusion.2
  291.4 5.3 fusion.216
  300.6 6.3 fusion.217
  310.5 10.0 broadcast_multiply_fusion.14
  320.4 5.4 fusion.220
  330.1 9.1 copy.129
  339.2 7.7 constant_dynamic-update-slice_fusion.2
  350.2 6.0 convolution_convert_fusion.1
  357.9 6.2 convolution_convert_fusion
  364.2 36.4 %while.48 = (s32[]{:T(128)}, f32[128,16,64]{0,2,1:T(8,128)S(1)}, bf16[2,1024,2048]{1,2,0:T(8,128)(2,1)}, s32[2]{0:T(128)S(1)}, s32[128]{0:T(128)S(1)}, /*index=5...) while((s32[]{:T(128)}, f32[128,16,64]{0,2,1:T(8,128)S(1)}, ...), condition=%wide.region_22.23_spmd.clone, body=%wide.region_21.22_spmd.clone.sunk | while | flops 818595328 | bytes 41707156 | solution.py:228
  374.6 7.8 fusion.242
  392.9 7.7 fusion.242
  400.9 299.6 %reduce-scatter.12.cloned.1.call-done = f32[128,2048]{1,0:T(8,128)} async-done(((f32[2048,2048]{1,0:T(8,128)}), f32[128,2048]{1,0:T(8,128)}) %reduce-scatter.12.cloned.1.call-update) | async-done | bytes 1048592 | tf_op jit(solution)/shard_map/reduce_scatter | solution.py:256
  717.0 38.6 %psum.79 = f32[3]{0:T(128)S(1)} all-reduce(f32[3]{0:T(128)S(1)} %pad_maximum_fusion.5), channel_id=1, replica_groups=mesh['ctx'=16,'fsdp'=2] {'ctx','fsdp'}, use_global_device_ids=true, to_apply=%region_58.59 | all-reduce | flops 3 | bytes 24 | tf_op jit(solution)/shard_map/psum | solution.py:176
  766.0 10.7 reduce-scatter.22.cloned.1.call-done
  777.7 17.9 reduce-scatter.14.cloned.1.call-done
  795.6 1067.7 %all-reduce.7 = (f32[512,3072]{1,0:T(8,128)}, f32[512,1024]{1,0:T(8,128)}, f32[512,4096]{1,0:T(8,128)}, f32[2048,1024]{1,0:T(8,128)}, f32[3,512]{1,0:T(4,128)}, ...) all-reduce(bf16[512,3072]{1,0:T(8,128)(2,1)} %reduce-scatter.14.clo, ...), channel_id=1, replica_groups=mesh['ctx'=16,'fsdp'=2] {'ctx'}, use_global_device_ids=true, to_apply=%region_29.30 | all-reduce | flops 6298632 | bytes 37800000 | tf_op jit(solution)/shard_map/psum | solution.py:299
  (291 shorter events, 138.4 us)
Async XLA Ops:
  7.2 20.4 %all-gather.6.cloned.1.call-start = ((), (), s32[]{:S(2)}) async-start(), calls=%async_computation.7 | async-start | bytes 9437184 | tf_op jit(solution)/shard_map/all_gather | solution.py:99
  7.9 135.7 %all-gather.8.cloned.1.call-start = ((), (), s32[]{:S(2)}) async-start(), calls=%async_computation.8 | async-start | bytes 8912896 | tf_op jit(solution)/shard_map/all_gather | solution.py:129
  11.8 19.7 %copy-start.35 = (f32[128]{0:T(128)}, f32[128]{0:T(128)S(1)}, u32[]{:S(2)}) copy-start(f32[128]{0:T(128)S(1)} %broadcast_multiply_fusion.12) | copy-start | bytes 1540
  12.0 214.6 %copy-start.29 = (f32[1,1024]{1,0:T(1,128)}, f32[1,1024]{1,0:T(1,128)S(1)}, u32[]{:S(2)}) copy-start(f32[1,1024]{1,0:T(1,128)S(1)} %get-tuple-element.858) | copy-start | bytes 12292
  12.1 188.7 %copy-start.33 = (f32[1,1024]{1,0:T(1,128)}, f32[1,1024]{1,0:T(1,128)S(1)}, u32[]{:S(2)}) copy-start(f32[1,1024]{1,0:T(1,128)S(1)} %get-tuple-element.861) | copy-start | bytes 12292
  32.3 164.1 %all-gather.10.cloned.1.call-start = ((), (), s32[]{:S(2)}) async-start(), calls=%async_computation.9 | async-start | bytes 3145728 | tf_op jit(solution)/shard_map/all_gather | solution.py:100
  33.1 167.7 %all-gather.12.cloned.1.call-start = ((), (), s32[]{:S(2)}) async-start(), calls=%async_computation.10 | async-start | bytes 12582912 | tf_op jit(solution)/shard_map/all_gather | solution.py:101
  33.7 173.6 %all-gather.14.cloned.1.call-start = ((), (), s32[]{:S(2)}) async-start(), calls=%async_computation.11 | async-start | bytes 12582912 | tf_op jit(solution)/shard_map/all_gather | solution.py:102
  34.3 666.2 %reduce-scatter.12.cloned.1.call-start = ((), (), s32[]{:S(2)}) async-start(), calls=%async_computation.12 | async-start | bytes 17825792 | tf_op jit(solution)/shard_map/reduce_scatter | solution.py:256
  40.4 182.7 %copy-start.27 = (f32[4096]{0:T(1024)}, f32[4096]{0:T(1024)S(1)}, u32[]{:S(2)}) copy-start(f32[4096]{0:T(1024)S(1)} %convert_element_type.149) | copy-start | bytes 49156
  42.7 180.4 %copy-start.31 = (f32[4096]{0:T(1024)}, f32[4096]{0:T(1024)S(1)}, u32[]{:S(2)}) copy-start(f32[4096]{0:T(1024)S(1)} %convert_element_type.150) | copy-start | bytes 49156
  199.8 26.9 %copy-start.45 = (f32[128]{0:T(128)}, f32[128]{0:T(128)S(1)}, u32[]{:S(2)}) copy-start(f32[128]{0:T(128)S(1)} %broadcast_multiply_fusion.10) | copy-start | bytes 1540
  200.8 25.9 %copy-start.49 = (f32[128]{0:T(128)}, f32[128]{0:T(128)S(1)}, u32[]{:S(2)}) copy-start(f32[128]{0:T(128)S(1)} %add_rsqrt_fusion.1) | copy-start | bytes 1540
  347.0 412.7 %reduce-scatter.16.cloned.1.call-start = ((), (), s32[]{:S(2)}) async-start(), calls=%async_computation.14 | async-start | bytes 3145728 | tf_op jit(solution)/shard_map/reduce_scatter | solution.py:274
  349.9 409.8 %reduce-scatter.18.cloned.1.call-start = ((), (), s32[]{:S(2)}) async-start(), calls=%async_computation.15 | async-start | bytes 12582912 | tf_op jit(solution)/shard_map/reduce_scatter | solution.py:277
  356.3 403.4 %reduce-scatter.20.cloned.1.call-start = ((), (), s32[]{:S(2)}) async-start(), calls=%async_computation.16 | async-start | bytes 12582912 | tf_op jit(solution)/shard_map/reduce_scatter | solution.py:280
  364.1 401.0 %reduce-scatter.24.cloned.1.call-start = ((), (), s32[]{:S(2)}) async-start(), calls=%async_computation.18 | async-start | bytes 393216
  364.1 36.7 %copy-start.42 = (bf16[1024]{0:T(1024)(128)(2,1)S(1)}, bf16[1024]{0:T(1024)(128)(2,1)}, u32[]{:S(2)}) copy-start(bf16[1024]{0:T(1024)(128)(2,1)} %get-tuple-element.772) | copy-start | bytes 6148
  364.1 36.7 %copy-start.57 = (bf16[1024]{0:T(1024)(128)(2,1)S(1)}, bf16[1024]{0:T(1024)(128)(2,1)}, u32[]{:S(2)}) copy-start(bf16[1024]{0:T(1024)(128)(2,1)} %get-tuple-element.770) | copy-start | bytes 6148
  364.1 36.7 %copy-start.41 = (bf16[1024]{0:T(1024)(128)(2,1)S(1)}, bf16[1024]{0:T(1024)(128)(2,1)}, u32[]{:S(2)}) copy-start(bf16[1024]{0:T(1024)(128)(2,1)} %get-tuple-element.753) | copy-start | bytes 6148
  364.2 36.8 %copy-start.56 = (bf16[1024]{0:T(1024)(128)(2,1)S(1)}, bf16[1024]{0:T(1024)(128)(2,1)}, u32[]{:S(2)}) copy-start(bf16[1024]{0:T(1024)(128)(2,1)} %get-tuple-element.769) | copy-start | bytes 6148
  400.6 301.2 %copy-start.5 = (bf16[1,128,1024]{2,1,0:T(8,128)(2,1)S(1)}, bf16[1,128,1024]{2,1,0:T(8,128)(2,1)}, u32[]{:S(2)}) copy-start(bf16[1,128,1024]{2,1,0:T(8,128)(2,1)} %param.18) | copy-start | bytes 786436
  400.6 301.2 %copy-start.24 = (f32[1,1024]{1,0:T(1,128)S(1)}, f32[1,1024]{1,0:T(1,128)}, u32[]{:S(2)}) copy-start(f32[1,1024]{1,0:T(1,128)} %copy-done.23) | copy-start | bytes 12292
  400.6 301.2 %copy-start.36 = (f32[128]{0:T(128)S(1)}, f32[128]{0:T(128)}, u32[]{:S(2)}) copy-start(f32[128]{0:T(128)} %copy-done.35) | copy-start | bytes 1540
  400.6 301.2 %copy-start.38 = (f32[128]{0:T(128)S(1)}, f32[128]{0:T(128)}, u32[]{:S(2)}) copy-start(f32[128]{0:T(128)} %copy-done.37) | copy-start | bytes 1540
  707.9 68.8 %reduce-scatter.22.cloned.1.call-start = ((), (), s32[]{:S(2)}) async-start(), calls=%async_computation.17 | async-start | bytes 393216
  708.9 86.7 %reduce-scatter.14.cloned.1.call-start = ((), (), s32[]{:S(2)}) async-start(), calls=%async_computation.13 | async-start | bytes 9437184 | tf_op jit(solution)/shard_map/reduce_scatter | solution.py:271
  713.6 42.1 %copy-start.39 = (bf16[4096]{0:T(1024)(128)(2,1)S(1)}, bf16[4096]{0:T(1024)(128)(2,1)}, u32[]{:S(2)}) copy-start(bf16[4096]{0:T(1024)(128)(2,1)} %get-tuple-element.749) | copy-start | bytes 24580
  713.6 42.1 %copy-start.40 = (bf16[4096]{0:T(1024)(128)(2,1)S(1)}, bf16[4096]{0:T(1024)(128)(2,1)}, u32[]{:S(2)}) copy-start(bf16[4096]{0:T(1024)(128)(2,1)} %get-tuple-element.752) | copy-start | bytes 24580
  713.6 42.1 %copy-start.55 = (bf16[16]{0:T(256)(128)(2,1)S(1)}, bf16[16]{0:T(256)(128)(2,1)}, u32[]{:S(2)}) copy-start(bf16[16]{0:T(256)(128)(2,1)} %get-tuple-element.759) | copy-start | bytes 100
  713.6 46.1 %copy-start.13 = (f32[128,1024]{1,0:T(8,128)S(1)}, f32[128,1024]{1,0:T(8,128)}, u32[]{:S(2)}) copy-start(f32[128,1024]{1,0:T(8,128)} %copy-done.12) | copy-start | bytes 1572868
  759.7 35.9 %copy-start.22 = (bf16[512,1024]{1,0:T(8,128)(2,1)S(1)}, bf16[512,1024]{1,0:T(8,128)(2,1)}, u32[]{:S(2)}) copy-start(bf16[512,1024]{1,0:T(8,128)(2,1)} %reduce-scatter.16.cloned.1.call-done) | copy-start | bytes 3145732
  (44 other events, 228.0 us)
Sparse Core Ops, SparseCore 0:
  9.6 17.9 all-gather.5
  32.5 111.1 all-gather.7
  145.2 11.0 all-gather.9
  157.7 21.0 all-gather.11
  180.1 21.0 all-gather.13
  347.0 353.4 reduce-scatter.11
  703.3 10.1 reduce-scatter.15
  716.4 17.6 reduce-scatter.17
  736.3 17.6 reduce-scatter.19
  756.1 8.8 reduce-scatter.23
  767.8 8.8 reduce-scatter.21
  779.4 16.0 reduce-scatter.13
where the time goes:
time: 1870 us
  blocking collectives  1120 us (60%)
  waiting for transfers between devices  451 us (24%)
  matrix products  136 us (7%)
  local copies, waits for them, and re-layouts  102 us (5%)
  other arithmetic  38.7 us (2%)
    psum x1, blocking collectives, local(): lax.psum((shard_grads[0], shard_grads[1], shard_grads[2], shard_grads[3],...  1070 us
    reduce_scatter x1, waiting for transfers between devices, local(): lax.psum_scatter(lax.map(key_term, sub_firsts).reshape(n_rows, 2 * model_...  300 us
    all_gather x1, waiting for transfers between devices, local(): fetched = lax.all_gather(keys_values, 'ctx', axis=0, tiled=True)  101 us
    psum x1, blocking collectives, local(): lax.psum(jnp.stack([jnp.sum(result * result), jnp.sum(attn_out * attn_out...  38.6 us
  transfers between devices with their start and end apart: 12, of which 6 were waited for; matrix products, arithmetic and copies ran while one was open for 7% of the time, Pallas kernels for 0%

commit v1 on v0

--- a/solution.py
+++ b/solution.py
@@ -173,11 +173,14 @@
     mixed_in = (norm_mid * mid_gains + mid_biases).astype(jnp.bfloat16)
     ffn_out = jnp.dot(mixed_in, fc2_full, preferred_element_type=jnp.float32)
     result = middle + ffn_out
-    sq_sums = lax.psum(
-        jnp.stack(
-            [jnp.sum(result * result), jnp.sum(attn_out * attn_out), jnp.sum(ffn_out * ffn_out)]
+    sq_sums = jnp.sum(
+        lax.all_gather(
+            jnp.stack(
+                [jnp.sum(result * result), jnp.sum(attn_out * attn_out), jnp.sum(ffn_out * ffn_out)]
+            ),
+            ("ctx", "fsdp"),
         ),
-        ("ctx", "fsdp"),
+        axis=0,
     )
     rms_values = jnp.sqrt(sq_sums / (stream_rows * lax.axis_size("fsdp") * model_width))
     grad_top = cotangent[0].astype(jnp.float32)

time: 1870 us -> 1870 us (level)
    psum x1 -> x0, blocking collectives: 38.6 us -> none  [local(): lax.psum(jnp.stack([jnp.sum(result * result), jnp.sum(attn_out * attn_out...]
    unnamed x2 -> x3, blocking collectives: 5.84 us -> 44.4 us
where the time goes in v1:
time: 1870 us
  blocking collectives  1120 us (60%)
  waiting for transfers between devices  451 us (24%)
  matrix products  136 us (7%)
  local copies, waits for them, and re-layouts  102 us (5%)
  other arithmetic  38.8 us (2%)
    psum x1, blocking collectives, local(): lax.psum((shard_grads[0], shard_grads[1], shard_grads[2], shard_grads[3],...  1070 us
    reduce_scatter x1, waiting for transfers between devices, local(): lax.psum_scatter(lax.map(key_term, sub_firsts).reshape(n_rows, 2 * model_...  300 us
    all_gather x1, waiting for transfers between devices, local(): fetched = lax.all_gather(keys_values, 'ctx', axis=0, tiled=True)  101 us
    unnamed x3, blocking collectives  44.4 us
  transfers between devices with their start and end apart: 12, of which 6 were waited for; matrix products, arithmetic and copies ran while one was open for 7% of the time, Pallas kernels for 0%

profile of v1, /device:TPU:26, one launch (start us, length us, event | category | flops | bytes accessed | tf_op | source)
XLA Modules:
  0.0 1870.3 jit_solution(6255520606601220638)
XLA Ops:
  12.1 15.5 all-gather.7.cloned.1.call-done
  43.0 100.6 %all-gather.9.cloned.1.call-done = bf16[2048,2048]{1,0:T(8,128)(2,1)} async-done(((bf16[128,2048]{1,0:T(8,128)(2,1)}), bf16[2048,2048]{1,0:T(8,128)(2,1)}) %all-gather.9.cloned.1.call-update) | async-done | bytes 8388624 | tf_op jit(solution)/shard_map/all_gather | solution.py:129
  143.6 12.0 copy.75
  155.7 40.6 %while.47 = (s32[]{:T(128)}, f32[128,16,64]{0,2,1:T(8,128)S(1)}, f32[128,16]{0,1:T(8,128)S(1)}, f32[128,16]{0,1:T(8,128)S(1)}, s32[2]{0:T(128)S(1)}, /*index=5*/...) while((s32[]{:T(128)}, f32[128,16,64]{0,2,1:T(8,128)S(1)}, ...), condition=%wide.region_7.8_spmd.clone, body=%wide.region_4.7_spmd.clone.sunk | while | flops 560786944 | bytes 81667752 | solution.py:157
  165.5 6.6 fusion.229
  185.8 6.3 fusion.229
  200.8 5.5 fusion.131
  207.5 6.7 multiply_reduce_fusion
  216.3 6.7 fusion.143
  230.1 116.8 %while.46 = (s32[]{:T(128)}, f32[2,1024,2048]{2,1,0:T(8,128)}, s32[2]{0:T(128)S(1)}, s32[128]{0:T(128)S(1)}, bf16[2048,2048]{1,0:T(8,128)(2,1)}, /*index=5*/bf16...) while((s32[]{:T(128)}, f32[2,1024,2048]{2,1,0:T(8,128)}, ...), condition=%wide.region_24.25_spmd.clone, body=%wide.region_23.24_spmd.clone.sunk | while | flops 1098302976 | bytes 123111664 | solution.py:260
  233.2 5.3 fusion.216
  242.4 6.3 fusion.217
  252.3 10.0 broadcast_multiply_fusion.14
  262.2 5.4 fusion.220
  271.9 9.1 copy.130
  281.0 7.7 constant_dynamic-update-slice_fusion.2
  291.4 5.3 fusion.216
  300.6 6.3 fusion.217
  310.5 10.0 broadcast_multiply_fusion.14
  320.4 5.4 fusion.220
  330.1 9.1 copy.130
  339.2 7.7 constant_dynamic-update-slice_fusion.2
  350.2 6.0 convolution_convert_fusion.1
  357.9 6.2 convolution_convert_fusion
  364.2 36.4 %while.48 = (s32[]{:T(128)}, f32[128,16,64]{0,2,1:T(8,128)S(1)}, bf16[2,1024,2048]{1,2,0:T(8,128)(2,1)}, s32[2]{0:T(128)S(1)}, s32[128]{0:T(128)S(1)}, /*index=5...) while((s32[]{:T(128)}, f32[128,16,64]{0,2,1:T(8,128)S(1)}, ...), condition=%wide.region_22.23_spmd.clone, body=%wide.region_21.22_spmd.clone.sunk | while | flops 818595328 | bytes 41707156 | solution.py:231
  374.6 7.8 fusion.242
  392.9 7.7 fusion.242
  400.9 299.6 %reduce-scatter.12.cloned.1.call-done = f32[128,2048]{1,0:T(8,128)} async-done(((f32[2048,2048]{1,0:T(8,128)}), f32[128,2048]{1,0:T(8,128)}) %reduce-scatter.12.cloned.1.call-update) | async-done | bytes 1048592 | tf_op jit(solution)/shard_map/reduce_scatter | solution.py:259
  717.1 38.6 %all-reduce.1 = f32[96]{0:T(128)S(1)} all-reduce(f32[96]{0:T(128)S(1)} %maximum_dynamic-update-slice_fusion), channel_id=2, replica_groups=mesh['ctx'=16,'fsdp'=2] {'ctx','fsdp'}, use_global_device_ids=true, to_apply=%add.1 | all-reduce | flops 96 | bytes 768
  766.0 10.7 reduce-scatter.22.cloned.1.call-done
  777.7 17.9 reduce-scatter.14.cloned.1.call-done
  795.6 1067.7 %all-reduce.8 = (f32[512,3072]{1,0:T(8,128)}, f32[512,1024]{1,0:T(8,128)}, f32[512,4096]{1,0:T(8,128)}, f32[2048,1024]{1,0:T(8,128)}, f32[3,512]{1,0:T(4,128)}, ...) all-reduce(bf16[512,3072]{1,0:T(8,128)(2,1)} %reduce-scatter.14.clo, ...), channel_id=1, replica_groups=mesh['ctx'=16,'fsdp'=2] {'ctx'}, use_global_device_ids=true, to_apply=%region_29.30 | all-reduce | flops 6298632 | bytes 37800000 | tf_op jit(solution)/shard_map/psum | solution.py:302
  (294 shorter events, 138.4 us)
Async XLA Ops:
  7.2 20.4 %all-gather.7.cloned.1.call-start = ((), (), s32[]{:S(2)}) async-start(), calls=%async_computation.7 | async-start | bytes 9437184 | tf_op jit(solution)/shard_map/all_gather | solution.py:99
  7.9 135.7 %all-gather.9.cloned.1.call-start = ((), (), s32[]{:S(2)}) async-start(), calls=%async_computation.8 | async-start | bytes 8912896 | tf_op jit(solution)/shard_map/all_gather | solution.py:129
  11.8 19.7 %copy-start.35 = (f32[128]{0:T(128)}, f32[128]{0:T(128)S(1)}, u32[]{:S(2)}) copy-start(f32[128]{0:T(128)S(1)} %broadcast_multiply_fusion.12) | copy-start | bytes 1540
  12.0 214.6 %copy-start.29 = (f32[1,1024]{1,0:T(1,128)}, f32[1,1024]{1,0:T(1,128)S(1)}, u32[]{:S(2)}) copy-start(f32[1,1024]{1,0:T(1,128)S(1)} %get-tuple-element.858) | copy-start | bytes 12292
  12.1 188.7 %copy-start.33 = (f32[1,1024]{1,0:T(1,128)}, f32[1,1024]{1,0:T(1,128)S(1)}, u32[]{:S(2)}) copy-start(f32[1,1024]{1,0:T(1,128)S(1)} %get-tuple-element.861) | copy-start | bytes 12292
  32.3 164.1 %all-gather.11.cloned.1.call-start = ((), (), s32[]{:S(2)}) async-start(), calls=%async_computation.9 | async-start | bytes 3145728 | tf_op jit(solution)/shard_map/all_gather | solution.py:100
  33.1 167.7 %all-gather.13.cloned.1.call-start = ((), (), s32[]{:S(2)}) async-start(), calls=%async_computation.10 | async-start | bytes 12582912 | tf_op jit(solution)/shard_map/all_gather | solution.py:101
  33.7 173.6 %all-gather.15.cloned.1.call-start = ((), (), s32[]{:S(2)}) async-start(), calls=%async_computation.11 | async-start | bytes 12582912 | tf_op jit(solution)/shard_map/all_gather | solution.py:102
  34.3 666.2 %reduce-scatter.12.cloned.1.call-start = ((), (), s32[]{:S(2)}) async-start(), calls=%async_computation.12 | async-start | bytes 17825792 | tf_op jit(solution)/shard_map/reduce_scatter | solution.py:259
  40.4 182.7 %copy-start.27 = (f32[4096]{0:T(1024)}, f32[4096]{0:T(1024)S(1)}, u32[]{:S(2)}) copy-start(f32[4096]{0:T(1024)S(1)} %convert_element_type.149) | copy-start | bytes 49156
  42.7 180.4 %copy-start.31 = (f32[4096]{0:T(1024)}, f32[4096]{0:T(1024)S(1)}, u32[]{:S(2)}) copy-start(f32[4096]{0:T(1024)S(1)} %convert_element_type.150) | copy-start | bytes 49156
  199.8 26.9 %copy-start.45 = (f32[128]{0:T(128)}, f32[128]{0:T(128)S(1)}, u32[]{:S(2)}) copy-start(f32[128]{0:T(128)S(1)} %broadcast_multiply_fusion.10) | copy-start | bytes 1540
  200.8 25.9 %copy-start.49 = (f32[128]{0:T(128)}, f32[128]{0:T(128)S(1)}, u32[]{:S(2)}) copy-start(f32[128]{0:T(128)S(1)} %add_rsqrt_fusion.1) | copy-start | bytes 1540
  347.0 412.9 %reduce-scatter.16.cloned.1.call-start = ((), (), s32[]{:S(2)}) async-start(), calls=%async_computation.14 | async-start | bytes 3145728 | tf_op jit(solution)/shard_map/reduce_scatter | solution.py:277
  349.9 409.9 %reduce-scatter.18.cloned.1.call-start = ((), (), s32[]{:S(2)}) async-start(), calls=%async_computation.15 | async-start | bytes 12582912 | tf_op jit(solution)/shard_map/reduce_scatter | solution.py:280
  356.3 403.6 %reduce-scatter.20.cloned.1.call-start = ((), (), s32[]{:S(2)}) async-start(), calls=%async_computation.16 | async-start | bytes 12582912 | tf_op jit(solution)/shard_map/reduce_scatter | solution.py:283
  364.1 401.0 %reduce-scatter.24.cloned.1.call-start = ((), (), s32[]{:S(2)}) async-start(), calls=%async_computation.18 | async-start | bytes 393216
  364.1 36.7 %copy-start.42 = (bf16[1024]{0:T(1024)(128)(2,1)S(1)}, bf16[1024]{0:T(1024)(128)(2,1)}, u32[]{:S(2)}) copy-start(bf16[1024]{0:T(1024)(128)(2,1)} %get-tuple-element.772) | copy-start | bytes 6148
  364.1 36.7 %copy-start.57 = (bf16[1024]{0:T(1024)(128)(2,1)S(1)}, bf16[1024]{0:T(1024)(128)(2,1)}, u32[]{:S(2)}) copy-start(bf16[1024]{0:T(1024)(128)(2,1)} %get-tuple-element.770) | copy-start | bytes 6148
  364.1 36.7 %copy-start.41 = (bf16[1024]{0:T(1024)(128)(2,1)S(1)}, bf16[1024]{0:T(1024)(128)(2,1)}, u32[]{:S(2)}) copy-start(bf16[1024]{0:T(1024)(128)(2,1)} %get-tuple-element.753) | copy-start | bytes 6148
  364.2 36.8 %copy-start.56 = (bf16[1024]{0:T(1024)(128)(2,1)S(1)}, bf16[1024]{0:T(1024)(128)(2,1)}, u32[]{:S(2)}) copy-start(bf16[1024]{0:T(1024)(128)(2,1)} %get-tuple-element.769) | copy-start | bytes 6148
  400.6 301.2 %copy-start.5 = (bf16[1,128,1024]{2,1,0:T(8,128)(2,1)S(1)}, bf16[1,128,1024]{2,1,0:T(8,128)(2,1)}, u32[]{:S(2)}) copy-start(bf16[1,128,1024]{2,1,0:T(8,128)(2,1)} %param.18) | copy-start | bytes 786436
  400.6 301.2 %copy-start.24 = (f32[1,1024]{1,0:T(1,128)S(1)}, f32[1,1024]{1,0:T(1,128)}, u32[]{:S(2)}) copy-start(f32[1,1024]{1,0:T(1,128)} %copy-done.23) | copy-start | bytes 12292
  400.6 301.2 %copy-start.36 = (f32[128]{0:T(128)S(1)}, f32[128]{0:T(128)}, u32[]{:S(2)}) copy-start(f32[128]{0:T(128)} %copy-done.35) | copy-start | bytes 1540
  400.6 301.2 %copy-start.38 = (f32[128]{0:T(128)S(1)}, f32[128]{0:T(128)}, u32[]{:S(2)}) copy-start(f32[128]{0:T(128)} %copy-done.37) | copy-start | bytes 1540
  707.9 68.8 %reduce-scatter.22.cloned.1.call-start = ((), (), s32[]{:S(2)}) async-start(), calls=%async_computation.17 | async-start | bytes 393216
  708.9 86.7 %reduce-scatter.14.cloned.1.call-start = ((), (), s32[]{:S(2)}) async-start(), calls=%async_computation.13 | async-start | bytes 9437184 | tf_op jit(solution)/shard_map/reduce_scatter | solution.py:274
  713.6 42.2 %copy-start.39 = (bf16[4096]{0:T(1024)(128)(2,1)S(1)}, bf16[4096]{0:T(1024)(128)(2,1)}, u32[]{:S(2)}) copy-start(bf16[4096]{0:T(1024)(128)(2,1)} %get-tuple-element.749) | copy-start | bytes 24580
  713.6 42.2 %copy-start.40 = (bf16[4096]{0:T(1024)(128)(2,1)S(1)}, bf16[4096]{0:T(1024)(128)(2,1)}, u32[]{:S(2)}) copy-start(bf16[4096]{0:T(1024)(128)(2,1)} %get-tuple-element.752) | copy-start | bytes 24580
  713.6 42.2 %copy-start.55 = (bf16[16]{0:T(256)(128)(2,1)S(1)}, bf16[16]{0:T(256)(128)(2,1)}, u32[]{:S(2)}) copy-start(bf16[16]{0:T(256)(128)(2,1)} %get-tuple-element.759) | copy-start | bytes 100
  713.6 46.3 %copy-start.13 = (f32[128,1024]{1,0:T(8,128)S(1)}, f32[128,1024]{1,0:T(8,128)}, u32[]{:S(2)}) copy-start(f32[128,1024]{1,0:T(8,128)} %copy-done.12) | copy-start | bytes 1572868
  759.9 35.7 %copy-start.22 = (bf16[512,1024]{1,0:T(8,128)(2,1)S(1)}, bf16[512,1024]{1,0:T(8,128)(2,1)}, u32[]{:S(2)}) copy-start(bf16[512,1024]{1,0:T(8,128)(2,1)} %reduce-scatter.16.cloned.1.call-done) | copy-start | bytes 3145732
  (44 other events, 228.0 us)
Sparse Core Ops, SparseCore 0:
  9.6 17.9 all-gather.6
  32.5 111.1 all-gather.8
  145.2 11.0 all-gather.10
  157.7 21.0 all-gather.12
  180.1 21.0 all-gather.14
  347.0 353.4 reduce-scatter.11
  703.3 10.1 reduce-scatter.15
  716.4 17.6 reduce-scatter.17
  736.3 17.6 reduce-scatter.19
  756.1 8.8 reduce-scatter.23
  767.8 8.8 reduce-scatter.21
  779.4 16.0 reduce-scatter.13
